TPU v7x, 32 devices: a whole 2x2x4 slice. The times are simulated.
32 devices in a mesh: fsdp: 4 (over y, x), req: 8 (over z, core).
Axes of the slice: x: 2, y: 2, z: 4, core: 2. Of those that a mesh axis runs over, the one named last changes fastest.
Arguments:
- x_prompt: bfloat16 [8, 256, 2048], P('req', 'fsdp')
- x_suffix: bfloat16 [8, 4, 256, 2048], P('req', 'fsdp')
- norm_gain: float32 [2048], replicated, may hold values from 0.1 to 1.9
- w_query: bfloat16 [2048, 1024], P('fsdp', 'req')
- w_key: bfloat16 [2048, 512], P('fsdp', 'req')
- w_value: bfloat16 [2048, 512], P('fsdp', 'req'), may hold values from -0.125 to 0.125
- query_gain: float32 [128], replicated
- key_gain: float32 [128], replicated
- adapter_down: bfloat16 [8, 16, 2048], P('fsdp'), may hold values from -0.125 to 0.125
- adapter_up: bfloat16 [8, 16, 1024], P('fsdp'), may hold values from -1.5 to 1.5
- prompt_len: int32 [8], P('req'), may hold values from 64 to 256, as said below
- member_count: int32 [8], P('req'), may hold values from 2 to 4, as said below
- suffix_len: int32 [8, 4], P('req', 'fsdp'), may hold values from 128 to 256, as said below
- adapter_id: int32 [8, 4], P('req'), may hold values from 0 to 7
- holder_slot: int32 [8], replicated, may hold values from 0 to 7, each once
Outputs:
- prompt_out: bfloat16 [8, 256, 1024], P('req', 'fsdp')
- suffix_out: bfloat16 [8, 4, 256, 1024], P('req', 'fsdp')
Inputs may be any that keep to these rules, and one draw needn't show every extreme that they name: `prompt_len`: some group's prompt has exactly 256 positions. `member_count`: some group is full. `suffix_len`: some member's suffix has exactly 256 tokens. `holder_slot`: each adapter has its own storage row.
All inputs are finite; a program needn't handle non-finite values.
Results may differ from a plain program's by a relative error of at most 0.0055.
The roundings to bfloat16 on the way count: a program that leaves them out, or rounds other values in their place, can miss the bound.
Values may be sent and summed in bfloat16 or wider, within the bound.
No kernel may reach another device: no remote copies, remote signals or barrier semaphores. Data moves between devices by JAX's collectives and lax.ppermute only.
A program may use at most 64 MiB of HBM per device.

v0:
```python
import jax
import jax.numpy as jnp
from jax import lax
from jax.sharding import PartitionSpec as P

epsilon = 1e-06
rope_base = 1000000.0
masked_low = -1e30


def norm_rows(values, gain_vector):
    return (
        values
        * lax.rsqrt(jnp.mean(values * values, axis=-1, keepdims=True) + epsilon)
        * gain_vector
    )


def rotate(heads_in, positions):
    half_dim = heads_in.shape[-1] // 2
    frequency = rope_base ** (-jnp.arange(half_dim).astype(jnp.float32) / half_dim)
    angles = positions.astype(jnp.float32)[:, None] * frequency[None, :]
    cosine = jnp.cos(angles)[:, None, :]
    sine = jnp.sin(angles)[:, None, :]
    first_half = heads_in[..., :half_dim]
    second_half = heads_in[..., half_dim:]
    return jnp.concatenate(
        [first_half * cosine - second_half * sine, second_half * cosine + first_half * sine],
        axis=-1,
    )


def shape_heads(flat_rows, gain_vector, positions, head_dim):
    per_head = flat_rows.reshape(flat_rows.shape[0], flat_rows.shape[1] // head_dim, head_dim)
    return rotate(norm_rows(per_head, gain_vector), positions)


def update(carried, scores, allowed, value_heads, pattern):
    running, denominator, summed_output = carried
    masked = jnp.where(allowed, scores, masked_low)
    newest = jnp.maximum(running, jnp.max(masked, axis=-1))
    weights = jnp.where(allowed, jnp.exp(scores - newest[..., None]), 0.0)
    factor = jnp.exp(running - newest)
    denominator = denominator * factor + jnp.sum(weights, axis=-1)
    summed_output = summed_output * factor[..., None] + jnp.einsum(
        pattern, weights.astype(jnp.bfloat16), value_heads, preferred_element_type=jnp.float32
    )
    return (newest, denominator, summed_output)


def shards(
    x_prompt,
    x_suffix,
    norm_gain,
    w_query,
    w_key,
    w_value,
    query_gain,
    key_gain,
    adapter_down,
    adapter_up,
    prompt_len,
    member_count,
    suffix_len,
    adapter_id,
    holder_slot,
):
    fsdp_rank = lax.axis_index("fsdp")
    req_count = lax.axis_size("req")
    pr_rows = x_prompt.shape[1]
    mem_dev = x_suffix.shape[1]
    suf_rows = x_suffix.shape[2]
    model_width = x_prompt.shape[2]
    head_dim = query_gain.shape[0]
    q_cols = w_query.shape[1] * req_count
    kv_cols = w_key.shape[1] * req_count
    kv_heads = kv_cols // head_dim
    group_size = q_cols // kv_cols
    row_count = pr_rows + mem_dev * suf_rows
    prompt_total = prompt_len[0]
    tokens = jnp.concatenate(
        [x_prompt[0], x_suffix[0].reshape(mem_dev * suf_rows, model_width)], axis=0
    )
    normed = norm_rows(tokens.astype(jnp.float32), norm_gain).astype(jnp.bfloat16)
    full_q, full_k, full_v = (
        lax.all_gather(w_query, "req", axis=1, tiled=True),
        lax.all_gather(w_key, "req", axis=1, tiled=True),
        lax.all_gather(w_value, "req", axis=1, tiled=True),
    )
    pieces = (
        lax.all_gather(full_q, "fsdp", axis=0, tiled=True),
        lax.all_gather(full_k, "fsdp", axis=0, tiled=True),
        lax.all_gather(full_v, "fsdp", axis=0, tiled=True),
    )
    base_q, base_k, base_v = tuple(
        (
            jnp.dot(normed, weight_piece, preferred_element_type=jnp.float32)
            for weight_piece in pieces
        )
    )
    member_ids = adapter_id[0]
    store_rows = holder_slot.shape[0]
    lookup = jnp.where(
        member_ids[:, None] == jnp.arange(store_rows)[None, :], holder_slot[None, :], 0
    )
    storage = jnp.sum(lookup, axis=1)
    store_down, store_up = (
        lax.all_gather(adapter_down, "fsdp", axis=0, tiled=True),
        lax.all_gather(adapter_up, "fsdp", axis=0, tiled=True),
    )
    mine = lax.dynamic_slice_in_dim(storage, fsdp_rank * mem_dev, mem_dev)
    select_down_matrix = jnp.take(store_down, mine, axis=0)
    select_up_matrix = jnp.take(store_up, mine, axis=0)
    suffix_input_rows = normed[pr_rows:].reshape(mem_dev, suf_rows, model_width)
    reduced_rank_rows = jnp.einsum(
        "bve,bfe->bvf", suffix_input_rows, select_down_matrix, preferred_element_type=jnp.float32
    ).astype(jnp.bfloat16)
    adapter_delta = jnp.einsum(
        "wge,wet->wgt", reduced_rank_rows, select_up_matrix, preferred_element_type=jnp.float32
    )
    query_full = jnp.concatenate(
        [base_q[:pr_rows], base_q[pr_rows:] + adapter_delta.reshape(mem_dev * suf_rows, q_cols)],
        axis=0,
    )
    prompt_pos = fsdp_rank * pr_rows + jnp.arange(pr_rows)
    suffix_pos = prompt_total + jnp.tile(jnp.arange(suf_rows), mem_dev)
    positions = jnp.concatenate([prompt_pos, suffix_pos])
    queries = (
        shape_heads(query_full, query_gain, positions, head_dim)
        .astype(jnp.bfloat16)
        .reshape(row_count, kv_heads, group_size, head_dim)
    )
    key_heads = shape_heads(base_k, key_gain, positions, head_dim).astype(jnp.bfloat16)
    value_heads = base_v.astype(jnp.bfloat16).reshape(row_count, kv_heads, head_dim)
    limits = jnp.concatenate([prompt_pos, jnp.full((mem_dev * suf_rows,), 2**30, jnp.int32)])
    score_scale = head_dim ** (-0.5)
    start_state = (
        jnp.full((row_count, kv_heads, group_size), masked_low, jnp.float32),
        jnp.zeros((row_count, kv_heads, group_size), jnp.float32),
        jnp.zeros((row_count, kv_heads, group_size, head_dim), jnp.float32),
    )
    prompt_k_flat = key_heads[:pr_rows].reshape(pr_rows, kv_cols)
    prompt_v_flat = value_heads[:pr_rows].reshape(pr_rows, kv_cols)
    piece_keys = lax.all_gather(prompt_k_flat, "fsdp", axis=0, tiled=True)
    piece_values = lax.all_gather(prompt_v_flat, "fsdp", axis=0, tiled=True)
    piece_rows = piece_keys.shape[0]
    key_pos = jnp.arange(piece_rows)
    allowed = (key_pos[None, :] < prompt_total) & (key_pos[None, :] <= limits[:, None])
    scores = (
        jnp.einsum(
            "rkgd,nkd->rkgn",
            queries,
            piece_keys.reshape(piece_rows, kv_heads, head_dim),
            preferred_element_type=jnp.float32,
        )
        * score_scale
    )
    carried = update(
        start_state,
        scores,
        allowed[:, None, None, :],
        piece_values.reshape(piece_rows, kv_heads, head_dim),
        "rkgn,nkd->rkgd",
    )
    suffix_state = tuple(
        (
            state_part[pr_rows:].reshape((mem_dev, suf_rows) + state_part.shape[1:])
            for state_part in carried
        )
    )
    suffix_q = queries[pr_rows:].reshape(mem_dev, suf_rows, kv_heads, group_size, head_dim)
    suffix_k = key_heads[pr_rows:].reshape(mem_dev, suf_rows, kv_heads, head_dim)
    suffix_v = value_heads[pr_rows:].reshape(mem_dev, suf_rows, kv_heads, head_dim)
    own_scores = (
        jnp.einsum("mskgd,mtkd->mskgt", suffix_q, suffix_k, preferred_element_type=jnp.float32)
        * score_scale
    )
    causal = jnp.arange(suf_rows)[None, :] <= jnp.arange(suf_rows)[:, None]
    suffix_state = update(
        suffix_state, own_scores, causal[None, :, None, None, :], suffix_v, "mskgt,mtkd->mskgd"
    )
    denominator = jnp.concatenate(
        [carried[1][:pr_rows], suffix_state[1].reshape(mem_dev * suf_rows, kv_heads, group_size)],
        axis=0,
    )
    summed_output = jnp.concatenate(
        [
            carried[2][:pr_rows],
            suffix_state[2].reshape(mem_dev * suf_rows, kv_heads, group_size, head_dim),
        ],
        axis=0,
    )
    attended = (summed_output / denominator[..., None]).reshape(row_count, q_cols)
    member_index = fsdp_rank * mem_dev + jnp.arange(mem_dev)
    suffix_ok = (member_index < member_count[0])[:, None] & (
        jnp.arange(suf_rows)[None, :] < suffix_len[0][:, None]
    )
    valid_rows = jnp.concatenate([prompt_pos < prompt_total, suffix_ok.reshape(mem_dev * suf_rows)])
    result = jnp.where(valid_rows[:, None], attended, 0.0).astype(jnp.bfloat16)
    return (result[:pr_rows][None], result[pr_rows:].reshape(1, mem_dev, suf_rows, q_cols))


def solution(mesh):
    return jax.shard_map(
        shards,
        mesh=mesh,
        in_specs=(
            P("req", "fsdp", None),
            P("req", "fsdp", None, None),
            P(),
            P("fsdp", "req"),
            P("fsdp", "req"),
            P("fsdp", "req"),
            P(),
            P(),
            P("fsdp", None, None),
            P("fsdp", None, None),
            P("req"),
            P("req"),
            P("req", "fsdp"),
            P("req", None),
            P(),
        ),
        out_specs=(P("req", "fsdp", None), P("req", "fsdp", None, None)),
        check_vma=False,
    )
```

profile of v0, /device:TPU:0, one launch (start us, length us, event | category | flops | bytes accessed | tf_op | source)
XLA Modules:
  0.0 200.5 jit_solution(7296874157899483863)
XLA Ops:
  7.3 0.7 all-gather.7.cloned.1.call-update
  8.0 18.0 %all_gather.37 = bf16[512,512]{0,1:T(8,128)(2,1)} all-gather(bf16[512,64]{0,1:T(8,128)(2,1)} %param.20), channel_id=1, replica_groups=mesh['fsdp'=4,'req'=8] {'req'}, dimensions={1}, use_global_device_ids=true | all-gather | bytes 589824 | tf_op jit(solution)/shard_map/all_gather | solution.py:88
  26.1 17.6 %all_gather.30 = bf16[512,512]{0,1:T(8,128)(2,1)} all-gather(bf16[512,64]{0,1:T(8,128)(2,1)} %param.19), channel_id=1, replica_groups=mesh['fsdp'=4,'req'=8] {'req'}, dimensions={1}, use_global_device_ids=true | all-gather | bytes 589824 | tf_op jit(solution)/shard_map/all_gather | solution.py:87
  43.8 0.5 all-gather.9.cloned.1.call-update
  44.3 0.2 select_reduce_fusion
  44.5 0.6 dynamic_slice.3
  49.0 10.7 %all_gather.36 = bf16[8,16,1024]{2,1,0:T(8,128)(2,1)} all-gather(bf16[2,16,1024]{2,1,0:T(8,128)(2,1)S(1)} %copy-done.7), channel_id=1, replica_groups=mesh['fsdp'=4,'req'=8] {'fsdp'}, dimensions={0}, use_global_device_ids=true | all-gather | bytes 327680 | tf_op jit(solution)/shard_map/all_gather | solution.py:109
  59.7 0.4 fusion
  60.1 15.3 %all_gather.35 = bf16[8,16,2048]{2,1,0:T(8,128)(2,1)} all-gather(bf16[2,16,2048]{2,1,0:T(8,128)(2,1)S(1)} %copy-done.6), channel_id=1, replica_groups=mesh['fsdp'=4,'req'=8] {'fsdp'}, dimensions={0}, use_global_device_ids=true | all-gather | bytes 655360 | tf_op jit(solution)/shard_map/all_gather | solution.py:108
  75.8 0.6 multiply_cosine_fusion
  76.5 0.4 fusion.2
  76.9 2.0 %all-gather.11.cloned.1.call-done = bf16[2048,512]{0,1:T(8,128)(2,1)} async-done(((bf16[512,512]{0,1:T(8,128)(2,1)}), bf16[2048,512]{0,1:T(8,128)(2,1)}) %all-gather.11.cloned.1.call-update) | async-done | bytes 2097168 | tf_op jit(solution)/shard_map/all_gather | solution.py:93
  78.9 2.5 %convolution_convert_fusion = bf16[320,512]{1,0:T(8,128)(2,1)S(1)} fusion(bf16[320,2048]{1,0:T(8,128)(2,1)S(1)} %fusion.2, bf16[2048,512]{0,1:T(8,128)(2,1)} %all-gather.11.cloned.1.call-done), kind=kOutput, calls=%fused_computation.37 | convolution fusion | flops 671252480 | bytes 3735552 | tf_op jit(solution)/shard_map/dot_general | solution.py:97
  81.4 0.9 copy.124
  82.2 33.7 %all-gather.5.cloned.1.call-done = bf16[2048,512]{0,1:T(8,128)(2,1)} async-done(((bf16[512,512]{0,1:T(8,128)(2,1)}), bf16[2048,512]{0,1:T(8,128)(2,1)}) %all-gather.5.cloned.1.call-update) | async-done | bytes 2097168 | tf_op jit(solution)/shard_map/all_gather | solution.py:92
  115.9 2.5 %fusion.64 = f32[320,512]{1,0:T(8,128)S(1)} fusion(bf16[320,2048]{1,0:T(8,128)(2,1)S(1)} %fusion.2, bf16[2048,512]{0,1:T(8,128)(2,1)} %all-gather.5.cloned.1.call-done), kind=kOutput, calls=%fused_computation.109 | convolution fusion | flops 671088640 | bytes 4063232 | tf_op jit(solution)/shard_map/dot_general | solution.py:97
  118.4 0.2 reshape.286
  118.6 0.4 multiply_reduce_fusion.1
  119.2 0.2 fusion.31
  119.4 0.3 subtract_convert_fusion.1
  119.8 10.2 %all_gather.32 = bf16[256,512]{1,0:T(8,128)(2,1)S(1)} all-gather(bf16[64,512]{1,0:T(8,128)(2,1)S(1)} %copy_bitcast_fusion), channel_id=1, replica_groups=mesh['fsdp'=4,'req'=8] {'fsdp'}, dimensions={0}, use_global_device_ids=true | all-gather | bytes 327680 | tf_op jit(solution)/shard_map/all_gather | solution.py:144
  130.1 0.9 copy.97
  130.9 10.5 %all_gather.39 = bf16[256,512]{1,0:T(8,128)(2,1)S(1)} all-gather(bf16[64,512]{1,0:T(8,128)(2,1)S(1)} %slice-done), channel_id=1, replica_groups=mesh['fsdp'=4,'req'=8] {'fsdp'}, dimensions={0}, use_global_device_ids=true | all-gather | bytes 327680 | tf_op jit(solution)/shard_map/all_gather | solution.py:145
  141.5 0.8 reshape.290
  142.2 30.4 %all-gather.9.cloned.1.call-done = bf16[2048,1024]{1,0:T(8,128)(2,1)} async-done(((bf16[512,1024]{1,0:T(8,128)(2,1)}), bf16[2048,1024]{1,0:T(8,128)(2,1)}) %all-gather.9.cloned.1.call-update) | async-done | bytes 4194320 | tf_op jit(solution)/shard_map/all_gather | solution.py:91
  172.6 4.8 %fusion.65 = f32[320,1024]{1,0:T(8,128)} fusion(bf16[320,2048]{1,0:T(8,128)(2,1)S(1)} %fusion.2, bf16[2048,1024]{1,0:T(8,128)(2,1)} %all-gather.9.cloned.1.call-done), kind=kOutput, calls=%fused_computation.110 | convolution fusion | flops 1342177280 | bytes 6815744 | tf_op jit(solution)/shard_map/dot_general | solution.py:97
  177.4 1.7 slice.99
  179.1 2.2 %convolution_add_fusion = f32[256,1024]{1,0:T(8,128)S(1)} fusion(bf16[320,2048]{1,0:T(8,128)(2,1)S(1)} %fusion.2, f32[320,1024]{1,0:T(8,128)} %fusion.65, bf16[8,16,2048]{2,1,0:T(8,128)(2,1)} %all_gather.35, s32[]{:T(128)} %bitcast.10, pred[]{:T(512)} %bitcast.9, bf16[8,16,1024]{2,1,0:T(8,128)(2,1)} %all_gather.36), kind=kOutput, calls=%fused_computation.25 | convolution fusion | flops 25481216 | bytes 3246080 | tf_op jit(solution)/shard_map/wge,wet->wgt/dot_general | solution.py:118
  181.3 1.1 maximum_bitcast_fusion
  182.4 0.3 copy.128
  182.7 0.4 multiply_reduce_fusion
  183.2 0.2 copy.99
  183.4 0.4 multiply_multiply_fusion
  183.8 0.6 subtract_convert_fusion
  184.5 0.3 pad_maximum_fusion.1
  185.0 0.5 copy-done.3
  185.4 1.0 fusion.3
  186.4 1.1 fusion.9
  187.6 0.6 fusion.6
  188.3 0.5 fusion.11
  188.8 0.9 fusion.15
  189.8 1.0 fusion.21
  190.7 0.3 copy.109
  191.1 0.2 copy.123
  191.4 0.5 fusion.14
  191.9 0.2 slice_bitcast_fusion
  192.1 0.8 copy.111
  192.9 1.0 copy.112
  (62 shorter events, 1.5 us)
Async XLA Ops:
  7.2 37.1 %copy-start.11 = (s32[8]{0:T(128)S(1)}, s32[8]{0:T(128)}, u32[]{:S(2)}) copy-start(s32[8]{0:T(128)} %param.29) | copy-start | bytes 100
  7.2 37.1 %copy-start.12 = (s32[1,4]{1,0:T(1,128)S(1)}, s32[1,4]{1,0:T(1,128)}, u32[]{:S(2)}) copy-start(s32[1,4]{1,0:T(1,128)} %param.28) | copy-start | bytes 52
  7.2 41.8 %copy-start.7 = (bf16[2,16,1024]{2,1,0:T(8,128)(2,1)S(1)}, bf16[2,16,1024]{2,1,0:T(8,128)(2,1)}, u32[]{:S(2)}) copy-start(bf16[2,16,1024]{2,1,0:T(8,128)(2,1)} %param.24) | copy-start | bytes 196612
  7.2 52.5 %copy-start = (bf16[1,1,256,2048]{3,2,1,0:T(8,128)(2,1)S(1)}, bf16[1,1,256,2048]{3,2,1,0:T(8,128)(2,1)}, u32[]{:S(2)}) copy-start(bf16[1,1,256,2048]{3,2,1,0:T(8,128)(2,1)} %param.16) | copy-start | bytes 3145732
  7.2 52.5 %copy-start.1 = (bf16[1,64,2048]{2,1,0:T(8,128)(2,1)S(1)}, bf16[1,64,2048]{2,1,0:T(8,128)(2,1)}, u32[]{:S(2)}) copy-start(bf16[1,64,2048]{2,1,0:T(8,128)(2,1)} %param.15) | copy-start | bytes 786436
  7.2 36.6 %all-gather.7.cloned.1.call-start = ((), (), s32[]{:S(2)}) async-start(), calls=%async_computation.1 | async-start | bytes 1179648 | tf_op jit(solution)/shard_map/all_gather | solution.py:86
  7.9 70.9 %all-gather.11.cloned.1.call-start = ((), (), s32[]{:S(2)}) async-start(), calls=%async_computation.3 | async-start | bytes 2621440 | tf_op jit(solution)/shard_map/all_gather | solution.py:93
  26.0 34.1 %copy-start.6 = (bf16[2,16,2048]{2,1,0:T(8,128)(2,1)S(1)}, bf16[2,16,2048]{2,1,0:T(8,128)(2,1)}, u32[]{:S(2)}) copy-start(bf16[2,16,2048]{2,1,0:T(8,128)(2,1)} %param.23) | copy-start | bytes 393220
  26.0 89.9 %all-gather.5.cloned.1.call-start = ((), (), s32[]{:S(2)}) async-start(), calls=%async_computation | async-start | bytes 2621440 | tf_op jit(solution)/shard_map/all_gather | solution.py:92
  43.7 32.8 %copy-start.8 = (f32[2048]{0:T(1024)S(1)}, f32[2048]{0:T(1024)}, u32[]{:S(2)}) copy-start(f32[2048]{0:T(1024)} %param.17) | copy-start | bytes 24580
  43.7 128.9 %all-gather.9.cloned.1.call-start = ((), (), s32[]{:S(2)}) async-start(), calls=%async_computation.2 | async-start | bytes 5242880 | tf_op jit(solution)/shard_map/all_gather | solution.py:91
  81.4 0.9 copy-start.4
  118.4 0.8 copy-start.9
  119.4 11.5 %slice-start = ((bf16[320,512]{1,0:T(8,128)(2,1)}), bf16[64,512]{1,0:T(8,128)(2,1)S(1)}, s32[]{:S(2)}) async-start(bf16[320,512]{1,0:T(8,128)(2,1)} %copy-done.4), calls=%async_computation.4 | async-start | bytes 131072 | tf_op jit(solution)/shard_map/slice | solution.py:143
  182.4 1.0 copy-start.10
  184.5 1.0 copy-start.3
  187.6 1.2 copy-start.5
  188.8 1.0 copy-start.2
Sparse Core Ops, SparseCore 0:
  9.6 29.3 all-gather.6
  40.9 37.9 all-gather.10
  80.7 35.1 all-gather.4
  117.6 54.9 all-gather.8
where the time goes:
time: 201 us; the launch traced here: 200 us
  blocking collectives  82.4 us (41%)
  waiting for transfers between devices  67.3 us (33%)
  between operations  18.2 us (9%)
  matrix products  15.3 us (8%)
  local copies, waits for them, and re-layouts  8.99 us (4%)
  other arithmetic  8.1 us (4%)
    all_gather x1, waiting for transfers between devices, shards(): lax.all_gather(full_k, 'fsdp', axis=0, tiled=True)  33.7 us
    all_gather x1, waiting for transfers between devices, shards(): lax.all_gather(full_q, 'fsdp', axis=0, tiled=True)  30.4 us
    all_gather x1, blocking collectives, shards(): lax.all_gather(w_value, 'req', axis=1, tiled=True)  18 us
    all_gather x1, blocking collectives, shards(): lax.all_gather(w_key, 'req', axis=1, tiled=True)  17.6 us
    all_gather x1, blocking collectives, shards(): lax.all_gather(adapter_down, 'fsdp', axis=0, tiled=True)  15.3 us
    all_gather x1, blocking collectives, shards(): lax.all_gather(adapter_up, 'fsdp', axis=0, tiled=True)  10.7 us
    all_gather x1, blocking collectives, shards(): piece_values = lax.all_gather(prompt_v_flat, 'fsdp', axis=0, tiled=True)  10.5 us
    all_gather x1, blocking collectives, shards(): piece_keys = lax.all_gather(prompt_k_flat, 'fsdp', axis=0, tiled=True)  10.2 us
  transfers between devices with their start and end apart: 4, of which 3 were waited for; matrix products, arithmetic and copies ran while one was open for 6% of the time, Pallas kernels for 0%

commit v1 on v0

--- a/solution.py
+++ b/solution.py
@@ -6,6 +6,11 @@
 epsilon = 1e-06
 rope_base = 1000000.0
 masked_low = -1e30
+draft_view = lambda local_array, x_local: jnp.split(
+    jax.lax.all_gather(jnp.concatenate([local_array, x_local], 1), "fsdp", axis=0, tiled=True),
+    [local_array.shape[1]],
+    1,
+)
 
 
 def norm_rows(values, gain_vector):
@@ -141,8 +146,7 @@
     )
     prompt_k_flat = key_heads[:pr_rows].reshape(pr_rows, kv_cols)
     prompt_v_flat = value_heads[:pr_rows].reshape(pr_rows, kv_cols)
-    piece_keys = lax.all_gather(prompt_k_flat, "fsdp", axis=0, tiled=True)
-    piece_values = lax.all_gather(prompt_v_flat, "fsdp", axis=0, tiled=True)
+    piece_keys, piece_values = draft_view(prompt_k_flat, prompt_v_flat)
     piece_rows = piece_keys.shape[0]
     key_pos = jnp.arange(piece_rows)
     allowed = (key_pos[None, :] < prompt_total) & (key_pos[None, :] <= limits[:, None])

time: 201 us -> 200 us (level)
  blocking collectives: 82.4 us -> 74.5 us
  local copies, waits for them, and re-layouts: 8.99 us -> 12.5 us
  waiting for transfers between devices: 67.3 us -> 70.8 us
    all_gather x2 -> x1, blocking collectives: 20.7 us -> 12.8 us  [jax.lax.all_gather(jnp.concatenate([local_array, x_local], 1), 'fsdp', ax...]
    all_gather x1, waiting for transfers between devices: 30.4 us -> 33.7 us  [shards(): lax.all_gather(full_q, 'fsdp', axis=0, tiled=True)]
  transfers between devices with their start and end apart: 4 -> 4, of which waited for: 3 -> 3; matrix products, arithmetic and copies ran while one was open for 6% -> 7% of each run, Pallas kernels for 0% -> 0%
where the time goes in v1:
time: 200 us
  blocking collectives  74.5 us (37%)
  waiting for transfers between devices  70.8 us (35%)
  between operations  18.2 us (9%)
  matrix products  15.4 us (8%)
  local copies, waits for them, and re-layouts  12.5 us (6%)
  other arithmetic  8.11 us (4%)
    all_gather x1, waiting for transfers between devices, shards(): lax.all_gather(full_k, 'fsdp', axis=0, tiled=True)  33.8 us
    all_gather x1, waiting for transfers between devices, shards(): lax.all_gather(full_q, 'fsdp', axis=0, tiled=True)  33.7 us
    all_gather x1, blocking collectives, shards(): lax.all_gather(w_value, 'req', axis=1, tiled=True)  18 us
    all_gather x1, blocking collectives, shards(): lax.all_gather(w_key, 'req', axis=1, tiled=True)  17.6 us
    all_gather x1, blocking collectives, shards(): lax.all_gather(adapter_down, 'fsdp', axis=0, tiled=True)  15.4 us
    all_gather x1, blocking collectives, jax.lax.all_gather(jnp.concatenate([local_array, x_local], 1), 'fsdp', ax...  12.8 us
    all_gather x1, blocking collectives, shards(): lax.all_gather(adapter_up, 'fsdp', axis=0, tiled=True)  10.7 us
    dot_general x3, matrix products, shards(): jnp.dot(normed, weight_piece, preferred_element_type=jnp.float32)  9.71 us
  transfers between devices with their start and end apart: 4, of which 3 were waited for; matrix products, arithmetic and copies ran while one was open for 7% of the time, Pallas kernels for 0%

profile of v1, /device:TPU:0, one launch (start us, length us, event | category | flops | bytes accessed | tf_op | source)
XLA Modules:
  0.0 199.7 jit_solution(6181205710699650206)
XLA Ops:
  7.3 0.7 all-gather.9.cloned.1.call-update
  8.0 18.0 %all_gather.29 = bf16[512,512]{0,1:T(8,128)(2,1)} all-gather(bf16[512,64]{0,1:T(8,128)(2,1)} %param.20), channel_id=1, replica_groups=mesh['fsdp'=4,'req'=8] {'req'}, dimensions={1}, use_global_device_ids=true | all-gather | bytes 589824 | tf_op jit(solution)/shard_map/all_gather | solution.py:93
  26.1 17.6 %all_gather.27 = bf16[512,512]{0,1:T(8,128)(2,1)} all-gather(bf16[512,64]{0,1:T(8,128)(2,1)} %param.19), channel_id=1, replica_groups=mesh['fsdp'=4,'req'=8] {'req'}, dimensions={1}, use_global_device_ids=true | all-gather | bytes 589824 | tf_op jit(solution)/shard_map/all_gather | solution.py:92
  43.8 0.5 all-gather.11.cloned.1.call-update
  44.3 0.2 select_reduce_fusion
  44.5 0.6 dynamic_slice.3
  49.0 10.7 %all_gather.35 = bf16[8,16,1024]{2,1,0:T(8,128)(2,1)} all-gather(bf16[2,16,1024]{2,1,0:T(8,128)(2,1)S(1)} %copy-done.7), channel_id=1, replica_groups=mesh['fsdp'=4,'req'=8] {'fsdp'}, dimensions={0}, use_global_device_ids=true | all-gather | bytes 327680 | tf_op jit(solution)/shard_map/all_gather | solution.py:114
  59.7 0.4 fusion
  60.1 15.4 %all_gather.34 = bf16[8,16,2048]{2,1,0:T(8,128)(2,1)} all-gather(bf16[2,16,2048]{2,1,0:T(8,128)(2,1)S(1)} %copy-done.6), channel_id=1, replica_groups=mesh['fsdp'=4,'req'=8] {'fsdp'}, dimensions={0}, use_global_device_ids=true | all-gather | bytes 655360 | tf_op jit(solution)/shard_map/all_gather | solution.py:113
  75.8 0.6 multiply_cosine_fusion
  76.5 0.4 fusion.2
  76.9 2.0 %all-gather.7.cloned.1.call-done = bf16[2048,512]{0,1:T(8,128)(2,1)} async-done(((bf16[512,512]{0,1:T(8,128)(2,1)}), bf16[2048,512]{0,1:T(8,128)(2,1)}) %all-gather.7.cloned.1.call-update) | async-done | bytes 2097168 | tf_op jit(solution)/shard_map/all_gather | solution.py:98
  78.9 2.5 %convolution_convert_fusion = bf16[320,512]{1,0:T(8,128)(2,1)S(1)} fusion(bf16[320,2048]{1,0:T(8,128)(2,1)S(1)} %fusion.2, bf16[2048,512]{0,1:T(8,128)(2,1)} %all-gather.7.cloned.1.call-done), kind=kOutput, calls=%fused_computation.37 | convolution fusion | flops 671252480 | bytes 3735552 | tf_op jit(solution)/shard_map/dot_general | solution.py:102
  81.4 0.7 copy-done.4
  82.1 33.8 %all-gather.5.cloned.1.call-done = bf16[2048,512]{0,1:T(8,128)(2,1)} async-done(((bf16[512,512]{0,1:T(8,128)(2,1)}), bf16[2048,512]{0,1:T(8,128)(2,1)}) %all-gather.5.cloned.1.call-update) | async-done | bytes 2097168 | tf_op jit(solution)/shard_map/all_gather | solution.py:97
  115.9 2.5 %fusion.66 = f32[320,512]{1,0:T(8,128)S(1)} fusion(bf16[320,2048]{1,0:T(8,128)(2,1)S(1)} %fusion.2, bf16[2048,512]{0,1:T(8,128)(2,1)} %all-gather.5.cloned.1.call-done), kind=kOutput, calls=%fused_computation.112 | convolution fusion | flops 671088640 | bytes 4063232 | tf_op jit(solution)/shard_map/dot_general | solution.py:102
  118.4 0.2 reshape.286
  118.6 0.4 multiply_reduce_fusion.1
  119.2 0.2 fusion.31
  119.4 0.3 subtract_convert_fusion.1
  120.0 12.8 %all_gather.31 = bf16[256,1024]{1,0:T(8,128)(2,1)S(1)} all-gather(bf16[64,1024]{1,0:T(8,128)(2,1)S(1)} %pad_maximum_fusion.3), channel_id=1, replica_groups=mesh['fsdp'=4,'req'=8] {'fsdp'}, dimensions={0}, use_global_device_ids=true | all-gather | bytes 655360 | tf_op jit(solution)/shard_map/all_gather | solution.py:10
  132.9 0.9 fusion.64
  133.7 1.7 reshape.288
  135.5 1.7 reshape.290
  137.2 0.8 copy.121
  138.0 33.7 %all-gather.11.cloned.1.call-done = bf16[2048,1024]{1,0:T(8,128)(2,1)} async-done(((bf16[512,1024]{1,0:T(8,128)(2,1)}), bf16[2048,1024]{1,0:T(8,128)(2,1)}) %all-gather.11.cloned.1.call-update) | async-done | bytes 4194320 | tf_op jit(solution)/shard_map/all_gather | solution.py:96
  171.8 4.8 %fusion.67 = f32[320,1024]{1,0:T(8,128)} fusion(bf16[320,2048]{1,0:T(8,128)(2,1)S(1)} %fusion.2, bf16[2048,1024]{1,0:T(8,128)(2,1)} %all-gather.11.cloned.1.call-done), kind=kOutput, calls=%fused_computation.113 | convolution fusion | flops 1342177280 | bytes 6815744 | tf_op jit(solution)/shard_map/dot_general | solution.py:102
  176.6 1.7 slice.100
  178.2 2.2 %convolution_add_fusion = f32[256,1024]{1,0:T(8,128)S(1)} fusion(bf16[320,2048]{1,0:T(8,128)(2,1)S(1)} %fusion.2, f32[320,1024]{1,0:T(8,128)} %fusion.67, bf16[8,16,2048]{2,1,0:T(8,128)(2,1)} %all_gather.34, s32[]{:T(128)} %bitcast.9, pred[]{:T(512)} %bitcast.8, bf16[8,16,1024]{2,1,0:T(8,128)(2,1)} %all_gather.35), kind=kOutput, calls=%fused_computation.25 | convolution fusion | flops 25481216 | bytes 3246080 | tf_op jit(solution)/shard_map/wge,wet->wgt/dot_general | solution.py:123
  180.5 1.1 maximum_bitcast_fusion
  181.6 0.3 copy.125
  181.9 0.4 multiply_reduce_fusion
  182.6 0.4 multiply_multiply_fusion
  183.0 0.6 subtract_convert_fusion
  183.8 0.3 pad_maximum_fusion.1
  184.1 0.5 copy-done.3
  184.5 1.0 fusion.3
  185.6 0.6 fusion.6
  186.3 1.1 fusion.9
  187.5 0.5 fusion.11
  188.1 0.9 fusion.15
  189.0 1.0 fusion.21
  190.0 0.3 copy.106
  190.3 0.2 copy.120
  190.6 0.5 fusion.14
  191.1 0.2 slice_bitcast_fusion
  191.4 1.0 copy.109
  192.4 0.8 copy.108
  (64 shorter events, 1.9 us)
Async XLA Ops:
  7.2 37.1 %copy-start.12 = (s32[1,4]{1,0:T(1,128)S(1)}, s32[1,4]{1,0:T(1,128)}, u32[]{:S(2)}) copy-start(s32[1,4]{1,0:T(1,128)} %param.28) | copy-start | bytes 52
  7.2 37.1 %copy-start.11 = (s32[8]{0:T(128)S(1)}, s32[8]{0:T(128)}, u32[]{:S(2)}) copy-start(s32[8]{0:T(128)} %param.29) | copy-start | bytes 100
  7.2 41.8 %copy-start.7 = (bf16[2,16,1024]{2,1,0:T(8,128)(2,1)S(1)}, bf16[2,16,1024]{2,1,0:T(8,128)(2,1)}, u32[]{:S(2)}) copy-start(bf16[2,16,1024]{2,1,0:T(8,128)(2,1)} %param.24) | copy-start | bytes 196612
  7.2 52.5 %copy-start.1 = (bf16[1,64,2048]{2,1,0:T(8,128)(2,1)S(1)}, bf16[1,64,2048]{2,1,0:T(8,128)(2,1)}, u32[]{:S(2)}) copy-start(bf16[1,64,2048]{2,1,0:T(8,128)(2,1)} %param.15) | copy-start | bytes 786436
  7.2 52.5 %copy-start = (bf16[1,1,256,2048]{3,2,1,0:T(8,128)(2,1)S(1)}, bf16[1,1,256,2048]{3,2,1,0:T(8,128)(2,1)}, u32[]{:S(2)}) copy-start(bf16[1,1,256,2048]{3,2,1,0:T(8,128)(2,1)} %param.16) | copy-start | bytes 3145732
  7.2 36.6 %all-gather.9.cloned.1.call-start = ((), (), s32[]{:S(2)}) async-start(), calls=%async_computation.2 | async-start | bytes 1179648 | tf_op jit(solution)/shard_map/all_gather | solution.py:91
  8.0 70.9 %all-gather.7.cloned.1.call-start = ((), (), s32[]{:S(2)}) async-start(), calls=%async_computation.1 | async-start | bytes 2621440 | tf_op jit(solution)/shard_map/all_gather | solution.py:98
  26.0 34.1 %copy-start.6 = (bf16[2,16,2048]{2,1,0:T(8,128)(2,1)S(1)}, bf16[2,16,2048]{2,1,0:T(8,128)(2,1)}, u32[]{:S(2)}) copy-start(bf16[2,16,2048]{2,1,0:T(8,128)(2,1)} %param.23) | copy-start | bytes 393220
  26.0 89.9 %all-gather.5.cloned.1.call-start = ((), (), s32[]{:S(2)}) async-start(), calls=%async_computation | async-start | bytes 2621440 | tf_op jit(solution)/shard_map/all_gather | solution.py:97
  43.7 32.8 %copy-start.8 = (f32[2048]{0:T(1024)S(1)}, f32[2048]{0:T(1024)}, u32[]{:S(2)}) copy-start(f32[2048]{0:T(1024)} %param.17) | copy-start | bytes 24580
  43.7 128.0 %all-gather.11.cloned.1.call-start = ((), (), s32[]{:S(2)}) async-start(), calls=%async_computation.3 | async-start | bytes 5242880 | tf_op jit(solution)/shard_map/all_gather | solution.py:96
  81.4 0.7 copy-start.4
  118.4 0.8 copy-start.9
  119.2 0.8 slice-start
  119.7 17.5 %slice-start.1 = ((bf16[320,512]{1,0:T(8,128)(2,1)}), bf16[256,512]{1,0:T(8,128)(2,1)S(1)}, s32[]{:S(2)}) async-start(bf16[320,512]{1,0:T(8,128)(2,1)} %copy-done.4), calls=%async_computation.5 | async-start | bytes 524288 | tf_op jit(solution)/shard_map/slice | solution.py:177
  181.6 1.0 copy-start.10
  183.6 1.0 copy-start.3
  186.3 1.7 copy-start.5
  188.1 1.0 copy-start.2
Sparse Core Ops, SparseCore 0:
  9.6 29.3 all-gather.8
  40.9 37.9 all-gather.6
  80.7 35.1 all-gather.4
  117.6 54.0 all-gather.10
